TPU v7x, 128 devices: a whole 4x4x4 slice. The times are simulated.
128 devices in a mesh: space: 8 (over x, core), tile: 16 (over y, z).
Axes of the slice: x: 4, y: 4, z: 4, core: 2. Of those that a mesh axis runs over, the one named last changes fastest.
Arguments:
- atom_feat: bfloat16 [2048, 128, 128], P(('space', 'tile')), may hold values from -6 to 6
- atom_pos: bfloat16 [2048, 3, 128], P(('space', 'tile')), may hold values from 0 to 4
- atom_counts: int32 [2048], P(('space', 'tile')), may hold values from 32 to 128
- atom_nbrs: int32 [2048, 4], P(('space', 'tile')), may hold values from 0 to 2047, as said below
- probe_pos: float32 [256, 3, 512], P(('space', 'tile')), may hold values from 0 to 4
- probe_target: float32 [256, 512], P(('space', 'tile')), may hold values from -6 to 6
- tile_blocks: int32 [256, 8], P(('space', 'tile')), may hold values from 0 to 2047, as said below
- atom_filter: bfloat16 [128, 1024], replicated, may hold values from -0.5 to 0.5
- probe_filter: bfloat16 [128, 1024], replicated, may hold values from -0.5 to 0.5
- mix_weight: bfloat16 [128, 128], replicated, may hold values from -0.5 to 0.5
- readout: float32 [128], replicated, may hold values from -0.5 to 0.5
Outputs:
- density: float32 [256, 512], P(('space', 'tile'))
- atom_filter_grad: float32 [128, 1024], replicated
- probe_filter_grad: float32 [128, 1024], replicated
- mix_grad: float32 [128, 128], replicated
- readout_grad: float32 [128], replicated
Inputs may be any that keep to these rules, and one draw needn't show every extreme that they name: `atom_nbrs`: block g lies on device g // 16 in the order space then tile. The 4 neighbours of a block lie on devices of the same tile index whose space index differs by at most one, cyclically: the first one lower, the second one higher, the third the same; they need not be distinct. `tile_blocks`: the 8 blocks of a tile are distinct and lie on devices of the tile's own space index. The tiles of one device read at most 2 distinct blocks from any one device, and exactly 2 from some device.
All inputs are finite; a program needn't handle non-finite values.
Results may differ from a plain program's by a relative error of at most 0.0061.
Values may be sent and summed in bfloat16 or wider, within the bound.
No kernel may reach another device: no remote copies, remote signals or barrier semaphores. Data moves between devices by JAX's collectives and lax.ppermute only.
A program may use at most 64 MiB of HBM per device.

v0:
```python
import functools
import math

import jax
import jax.numpy as jnp
import numpy as np
from jax import lax
from jax.experimental import pallas as pl
from jax.experimental.pallas import tpu as pltpu
from jax.sharding import PartitionSpec as P

BOTH = ("space", "tile")
F32 = jnp.float32
BF16 = jnp.bfloat16

CUTOFF = 6.0
SPACING = 0.75
SPREAD = 0.75
SOFT = 0.01
AUG = 16
READY = 5
MARK = 32.0


def envelope_terms(degree=4):
    top = CUTOFF * CUTOFF
    nodes = 0.5 * top * (1.0 - np.cos(np.pi * (np.arange(64) + 0.5) / 64))
    values = np.cos(np.pi * np.sqrt(nodes) / (2 * CUTOFF)) / (top - nodes)
    fit = np.polynomial.chebyshev.Chebyshev.fit(nodes, values, degree, domain=[0.0, top])
    return [float(c) for c in fit.convert(kind=np.polynomial.Polynomial).coef]


ENVELOPE = envelope_terms()


def radial_store(square, factor, filters, store):
    distance = square * lax.rsqrt(square)
    root = math.sqrt(factor)
    poly = jnp.full_like(square, ENVELOPE[-1] * root)
    for term in ENVELOPE[-2::-1]:
        poly = poly * square + term * root
    half = jnp.maximum(CUTOFF * CUTOFF - square, 0.0) * poly
    value = (half * half) * jnp.exp2(square * (-math.log2(math.e) / SPREAD**2))
    growth = jnp.exp2(distance * (2.0 * math.log2(math.e) * SPACING / SPREAD**2))
    for r in range(filters):
        store(r, value.astype(BF16))
        if r + 1 < filters:
            value = value * growth


def decay(r):
    return math.exp(-((r * SPACING / SPREAD) ** 2))


def sigmoid(values):
    return 1.0 / (1.0 + jnp.exp(-values))


def dot(a, b, contract):
    return lax.dot_general(a, b, ((contract[0:1], contract[1:2]), ((), ())), preferred_element_type=F32)


def stacked(rows):
    at = lax.broadcasted_iota(jnp.int32, (AUG, rows[0].shape[1]), 0)
    out = jnp.zeros(at.shape, F32)
    for i, row in enumerate(rows):
        out = jnp.where(at == i, row, out)
    return out.astype(BF16)


def pieces(values):
    high = values.astype(BF16).astype(F32)
    rest = values - high
    middle = rest.astype(BF16).astype(F32)
    return [high, middle, rest - middle]


def source_rows(x, y, z):
    unit = jnp.ones_like(x)
    return stacked([x, y, z] * 3 + pieces(x * x + y * y + z * z) + [unit] * 3)


def target_rows(x, y, z):
    unit = jnp.ones_like(x)
    parts = [pieces(-2.0 * row) for row in (x, y, z)]
    rows = [part[i] for i in range(3) for part in parts]
    return stacked(rows + [unit] * 3 + pieces(x * x + y * y + z * z + SOFT))


def setup_kernel(reads_ref, counts_ref, where_ref, early_ref, marked_ref, info_ref, asks):
    peers = early_ref.shape[0]
    blocks = where_ref.shape[1]
    width = where_ref.shape[2]
    tiles, reads = reads_ref.shape
    owners, spots = [], []
    for t in range(tiles):
        for k in range(reads):
            block = reads_ref[t, k]
            owners.append(lax.rem(lax.div(block, blocks), peers))
            spots.append(lax.rem(block, blocks))
    for i in range(2 * peers):
        asks[i] = 0
    for i, (owner, spot) in enumerate(zip(owners, spots)):
        rank = jnp.int32(0)
        for j in range(len(owners)):
            if j != i:
                rank = jnp.where((owners[j] == owner) & (spots[j] < spot), 1, rank)
        slot = owner * 2 + rank
        info_ref[0, i] = slot
        info_ref[1, i] = owner
        info_ref[2, i] = spot
        asks[slot] = spot
    line = lax.broadcasted_iota(jnp.int32, (blocks, width), 0)
    lane = lax.broadcasted_iota(jnp.int32, (blocks, width), 1)
    counts = jnp.zeros((blocks, width), jnp.int32)
    for i in range(blocks):
        counts = jnp.where(line == i, counts_ref[i], counts)
    for c in range(3):
        marked_ref[c] = jnp.where(lane < counts, where_ref[c].astype(F32), 2.0 * MARK).astype(BF16)
    lane = lax.broadcasted_iota(jnp.int32, (AUG, width), 1)
    for t in range(peers):
        for c in range(3):
            early_ref[t, c * blocks : (c + 1) * blocks, :] = where_ref[c]
        note = jnp.where(lane == 0, asks[2 * t], jnp.where(lane == 1, asks[2 * t + 1], 0))
        early_ref[t, 3 * blocks :, :] = note.astype(F32).astype(BF16)


def atom_kernel(peers, nbr_ref, lo_ref, own_ref, hi_ref, lo_pos, own_pos, hi_pos, weight_ref,
                sums_ref, slope_ref, done_ref, rows, masks, goals, feat, kern):
    b = pl.program_id(0)
    blocks, channels, width = own_ref.shape
    nbrs = feat.shape[1]
    filters = kern.shape[1]
    scale = (nbrs * width) ** -0.5

    @pl.when(b == 0)
    def _():
        for s, pos in enumerate((lo_pos, own_pos, hi_pos)):
            wide = [pos[c].astype(F32) for c in range(3)]
            there = wide[0] < MARK
            wide = [jnp.where(there, w, 0.0) for w in wide]
            masks[s] = there.astype(F32)
            for i in range(blocks):
                x, y, z = (w[i : i + 1, :] for w in wide)
                rows[s * blocks + i] = source_rows(x, y, z)
                if s == 1:
                    goals[i] = target_rows(x, y, z)

    def pick(slot, k, feats, s, index):
        mask = jnp.broadcast_to(masks[s, pl.ds(index, 1), :], (channels, width)).astype(BF16)
        feat[slot, k] = feats[index] * mask

    def prepare(slot, k, index):
        square = dot(rows[index], goals[jnp.minimum(b, blocks - 1)], (0, 0))

        def store(r, value):
            kern[slot, r, k * width : (k + 1) * width, :] = value

        radial_store(square, scale, filters, store)

    def finish(slot, r):
        feats = jnp.concatenate([feat[slot, k] for k in range(nbrs)], axis=1)
        kerns = jnp.concatenate([kern[slot, r], kern[slot, r + 1]], axis=1)
        part = dot(feats, kerns, (1, 0))
        for i in range(2):
            piece = part[:, i * width : (i + 1) * width] * decay(r + i)
            sums_ref[0, (r + i) * channels : (r + i + 1) * channels, :] = piece.astype(BF16)

    def last(at):
        sums = sums_ref[0]
        message = dot(weight_ref[...], sums, (1, 0))
        mask = masks[1, pl.ds(at, 1), :]
        gate = sigmoid(message)
        slope_ref[0] = gate * (1.0 + message * (1.0 - gate)) * mask
        done_ref[0] = ((own_ref[at].astype(F32) + message * gate) * mask).astype(BF16)

    def step(slot):
        at = jnp.minimum(b, blocks - 1)
        picked = [nbr_ref[k, at] for k in range(nbrs)]
        index = [lax.rem(block, blocks) for block in picked]
        space = [lax.div(block, blocks * peers) for block in picked]
        side = jnp.where(space[3] == space[2], 1, jnp.where(space[3] == space[0], 0, 2))
        sides = [0, 2, 1, side]
        pick(slot, 0, lo_ref, 0, index[0])
        pick(slot, 1, hi_ref, 2, index[1])
        pick(slot, 2, own_ref, 1, index[2])
        for s, feats in enumerate((lo_ref, own_ref, hi_ref)):
            @pl.when(side == s)
            def _():
                pick(slot, 3, feats, s, index[3])

        for k in range(nbrs):
            prepare(slot, k, sides[k] * blocks + index[k])
            finish(1 - slot, 2 * k)
        last(jnp.maximum(b - 1, 0))

    @pl.when(b % 2 == 0)
    def _():
        step(0)

    @pl.when(b % 2 == 1)
    def _():
        step(1)


def radial_block(rows, goals_ref, t, scale, filters, store):
    for at in range(goals_ref.shape[1]):
        square = dot(rows, goals_ref[t, at], (0, 0))
        radial_store(square, scale, filters, functools.partial(store, at))


def rows_kernel(info_ref, early_ref, probe_ref, rows_ref, goals_ref, kern_ref, places, held, left):
    blocks = (early_ref.shape[1] - AUG) // 3
    width = early_ref.shape[2]
    reads = rows_ref.shape[0] // goals_ref.shape[0]
    scale = (reads * width) ** -0.5
    places[...] = early_ref[...].astype(F32)
    for b in range(rows_ref.shape[0]):
        owner, spot = info_ref[1, b], info_ref[2, b]
        rows_ref[b] = source_rows(*(places[owner, pl.ds(c * blocks + spot, 1), :] for c in range(3)))
    for t in range(goals_ref.shape[0]):
        goal = target_rows(*(probe_ref[c, t : t + 1, :] for c in range(3)))
        for at in range(goals_ref.shape[1]):
            goals_ref[t, at] = goal[:, at * 128 : (at + 1) * 128]

    def leave(k):
        return pltpu.make_async_copy(held.at[k], kern_ref.at[k], left.at[k])

    for k in range(held.shape[0]):
        def store(at, r, value):
            held[k, r, at] = value

        radial_block(rows_ref[k], goals_ref, 0, scale, held.shape[1], store)
        leave(k).start()
    for k in range(held.shape[0]):
        leave(k).wait()


def probe_kernel(info_ref, ready_ref, rows_ref, goals_ref, reply_ref, goal_ref, weight_ref, mix_ref, read_ref,
                 density_ref, probe_ref, mixg_ref, readg_ref, back_ref,
                 first, second, arrived, sums, squashed, grads_mixed, grads_hidden, slopes, grads, total):
    _, channels, width = reply_ref.shape
    tiles, probes = goal_ref.shape
    filters, chunks = first.shape[:2]
    reads = rows_ref.shape[0] // tiles
    ready = ready_ref.shape[0]
    scale = (reads * width) ** -0.5
    kerns = (first, second)

    def fetch(k):
        return pltpu.make_async_copy(ready_ref.at[k], first.at[:, :, k * width : (k + 1) * width, :], arrived.at[k])

    for k in range(ready):
        fetch(k).start()
    line = lax.broadcasted_iota(jnp.int32, (channels, channels), 0)
    diagonal = line == lax.broadcasted_iota(jnp.int32, (channels, channels), 1)
    readout = jnp.sum(jnp.where(diagonal, read_ref[...], 0.0), axis=1, keepdims=True)
    total[...] = jnp.zeros_like(total)

    def radial(t, k):
        def store(at, r, value):
            kerns[t][r, at, pl.ds(pl.multiple_of(k * width, width), width), :] = value

        radial_block(rows_ref[t * reads + k], goals_ref, t, scale, filters, store)

    def forward(t):
        feats = jnp.concatenate([reply_ref[info_ref[0, t * reads + k]] for k in range(reads)], axis=1)
        for r in range(filters):
            for at in range(0, chunks, 2):
                right = jnp.concatenate([kerns[t][r, at], kerns[t][r, at + 1]], axis=1)
                part = (dot(feats, right, (1, 0)) * decay(r)).astype(BF16)
                for i in range(2):
                    sums[at + i, r * channels : (r + 1) * channels, :] = part[:, i * 128 : (i + 1) * 128]

    def halves(ref, at, value):
        for i in range(2):
            ref[at + i] = value[:, i * 128 : (i + 1) * 128]

    def middle(t):
        grad_read = jnp.zeros((channels, 1), F32)
        for at in range(0, chunks, 2):
            span = slice(at * 128, (at + 2) * 128)
            hidden = dot(weight_ref[...], jnp.concatenate([sums[at], sums[at + 1]], axis=1), (1, 0))
            gate = sigmoid(hidden)
            squash = (hidden * gate).astype(BF16)
            halves(squashed, at, squash)
            slopes[...] = gate * (1.0 + hidden * (1.0 - gate))
            mixed = dot(mix_ref[...], squash, (1, 0))
            outer_gate = sigmoid(mixed)
            outer = mixed * outer_gate
            density = jnp.sum(readout * outer, axis=0, keepdims=True)
            density_ref[t : t + 1, span] = density
            misfit = (density - goal_ref[t : t + 1, span]) * (1.0 / probes)
            grad_read = grad_read + jnp.sum(outer * misfit, axis=1, keepdims=True)
            grad_mixed = (readout * misfit * (outer_gate * (1.0 + mixed * (1.0 - outer_gate)))).astype(BF16)
            halves(grads_mixed, at, grad_mixed)
            halves(grads_hidden, at, (dot(mix_ref[...], grad_mixed, (0, 0)) * slopes[...]).astype(BF16))
        grad_read = jnp.sum(jnp.where(diagonal, grad_read, 0.0), axis=0, keepdims=True)

        def joined(ref):
            return jnp.concatenate([ref[at] for at in range(chunks)], axis=1)

        grad_hidden = joined(grads_hidden)
        grad_mix = dot(joined(grads_mixed), joined(squashed), (1, 1))
        grad_probe = dot(grad_hidden, joined(sums), (1, 1))
        if t == 0:
            readg_ref[...], mixg_ref[...], probe_ref[...] = grad_read, grad_mix, grad_probe
        else:
            readg_ref[...] += grad_read
            mixg_ref[...] += grad_mix
            probe_ref[...] += grad_probe
        for r in range(filters):
            part = dot(weight_ref[:, r * channels : (r + 1) * channels], grad_hidden, (0, 0)) * decay(r)
            part = part.astype(BF16)
            for at in range(chunks):
                grads[r * chunks + at] = part[:, at * 128 : (at + 1) * 128]

    def backward(t):
        all_grads = jnp.concatenate([grads[i] for i in range(filters * chunks)], axis=1)
        for k in range(0, reads, 2):
            lines = slice(k * width, (k + 2) * width)
            right = jnp.concatenate(
                [kerns[t][r, at, lines, :] for r in range(filters) for at in range(chunks)], axis=1
            )
            part = dot(all_grads, right, (1, 1))
            for i in range(2):
                slot = info_ref[0, t * reads + k + i]
                total[slot] += part[:, i * width : (i + 1) * width]

    @pl.loop(0, reads)
    def _(k):
        radial(1, k)

    @pl.loop(ready, reads)
    def _(k):
        radial(0, k)

    for k in range(ready):
        fetch(k).wait()
    for t in range(tiles):
        forward(t)
        middle(t)
        backward(t)
    back_ref[...] = total[...].astype(BF16)


def owner_kernel(asked_ref, back_ref, slope_ref, sums_ref, probe_ref, mix_ref, read_ref, out_ref, total, grads):
    step = pl.program_id(0)
    blocks, channels, width = slope_ref.shape
    columns = sums_ref.shape[1]
    across = probe_ref.shape[1] // width
    high = 8

    @pl.when(step == 0)
    def _():
        total[...] = jnp.zeros_like(total)

        def gather(i, carry):
            at = asked_ref[i]
            total[at] = total[at] + back_ref[i].astype(F32)
            return carry

        lax.fori_loop(0, back_ref.shape[0], gather, 0)
        for b in range(blocks):
            grads[b] = (total[b] * slope_ref[b]).astype(BF16)
        for i in range(channels // high):
            lines = slice(i * high, (i + 1) * high)
            for j in range(across):
                out_ref[i * across + j, high : 2 * high, :] = probe_ref[lines, j * width : (j + 1) * width].astype(BF16)
            out_ref[i, 2 * high :, :] = mix_ref[lines, :].astype(BF16)
        out_ref[channels // high, 2 * high :, :] = jnp.broadcast_to(read_ref[...], (high, width)).astype(BF16)
        for i in range(channels // high + 1, out_ref.shape[0]):
            out_ref[i, 2 * high :, :] = jnp.zeros((high, width), BF16)

    all_grads = jnp.concatenate([grads[b] for b in range(blocks)], axis=1)
    all_sums = jnp.concatenate([sums_ref[b] for b in range(blocks)], axis=1)
    part = dot(all_grads, all_sums, (1, 1)).astype(BF16)
    for i in range(channels // high):
        for j in range(columns // width):
            out_ref[i * across + step * (columns // width) + j, :high, :] = part[
                i * high : (i + 1) * high, j * width : (j + 1) * width
            ]


def spread_kernel(parts_ref, out_ref):
    mine = jnp.sum(parts_ref[...].astype(F32), axis=0, keepdims=True).astype(BF16)
    out_ref[...] = jnp.broadcast_to(mine, out_ref.shape)


def whole(shape):
    return pl.BlockSpec(shape, lambda *_: (0,) * len(shape))


def call(kernel, grid, prefetch, ins, in_specs, outs, out_specs, scratch, cost, limit=None):
    return pl.pallas_call(
        kernel,
        grid_spec=pltpu.PrefetchScalarGridSpec(
            num_scalar_prefetch=len(prefetch), grid=grid, in_specs=in_specs, out_specs=out_specs,
            scratch_shapes=scratch,
        ),
        out_shape=outs,
        cost_estimate=pl.CostEstimate(flops=cost[0], bytes_accessed=cost[1], transcendentals=cost[2]),
        compiler_params=pltpu.CompilerParams(vmem_limit_bytes=limit),
    )(*prefetch, *ins)


SMEM = pl.BlockSpec(memory_space=pltpu.SMEM)
VMEM = pl.BlockSpec(memory_space=pltpu.VMEM)


def plain(kernel, ins, in_specs, out_specs, outs, scratch, limit, cost=None):
    return pl.pallas_call(
        kernel, in_specs=in_specs, out_specs=out_specs, out_shape=outs, scratch_shapes=scratch,
        cost_estimate=cost and pl.CostEstimate(flops=cost[0], bytes_accessed=cost[1], transcendentals=cost[2]),
        compiler_params=pltpu.CompilerParams(vmem_limit_bytes=limit),
    )(*ins)


def reduced(chunks):
    sent = lax.all_to_all(chunks, BOTH, 0, 0, tiled=True)
    vmem = pl.BlockSpec(memory_space=pltpu.VMEM)
    totals = pl.pallas_call(
        spread_kernel, in_specs=[vmem], out_specs=vmem, out_shape=jax.ShapeDtypeStruct(sent.shape, BF16), name="spread",
        compiler_params=pltpu.CompilerParams(vmem_limit_bytes=4 << 20),
    )(sent)
    return lax.all_to_all(totals, BOTH, 0, 0, tiled=True)


def body(atom_feat, atom_pos, atom_counts, atom_nbrs, probe_pos, probe_target, tile_blocks, atom_filter, probe_filter,
         mix_weight, readout):
    blocks, channels, width = atom_feat.shape
    tiles, reads = tile_blocks.shape
    probes = probe_pos.shape[2]
    filters = atom_filter.shape[1] // channels
    peers = lax.axis_size("tile")
    spaces = lax.axis_size("space")
    devices = peers * spaces
    slots = peers * 2
    up = [(i, (i + 1) % spaces) for i in range(spaces)]
    down = [(i, (i - 1) % spaces) for i in range(spaces)]

    feat_lo = lax.ppermute(atom_feat, "space", up)
    feat_hi = lax.ppermute(atom_feat, "space", down)
    smem = pl.BlockSpec(memory_space=pltpu.SMEM)
    vmem = pl.BlockSpec(memory_space=pltpu.VMEM)
    where = jnp.transpose(atom_pos, (1, 0, 2))
    early, marked, info = pl.pallas_call(
        setup_kernel,
        in_specs=[smem, smem, vmem],
        out_specs=[vmem, vmem, smem],
        out_shape=(
            jax.ShapeDtypeStruct((peers, 3 * blocks + AUG, width), BF16),
            jax.ShapeDtypeStruct(where.shape, BF16),
            jax.ShapeDtypeStruct((3, tiles * reads), jnp.int32),
        ),
        scratch_shapes=[pltpu.SMEM((slots,), jnp.int32)],
        name="requests",
        compiler_params=pltpu.CompilerParams(vmem_limit_bytes=4 << 20),
    )(tile_blocks, atom_counts, where)
    pos_lo = lax.ppermute(marked, "space", up)
    pos_hi = lax.ppermute(marked, "space", down)
    early = lax.all_to_all(early, "tile", 0, 0, tiled=True)

    pairs = blocks * 4 * width * width

    def before(shape):
        return pl.BlockSpec((1, *shape[1:]), lambda b, *_: (jnp.maximum(b - 1, 0),) + (0,) * (len(shape) - 1))

    sums_shape = (blocks, filters * channels, width)
    sums, slope, done = call(
        functools.partial(atom_kernel, peers), (blocks + 1,), (atom_nbrs.T,),
        (feat_lo, atom_feat, feat_hi, pos_lo, marked, pos_hi, atom_filter),
        [whole(atom_feat.shape)] * 3 + [whole(marked.shape)] * 3 + [whole(atom_filter.shape)],
        (
            jax.ShapeDtypeStruct(sums_shape, BF16),
            jax.ShapeDtypeStruct(atom_feat.shape, F32),
            jax.ShapeDtypeStruct(atom_feat.shape, BF16),
        ),
        [before(sums_shape), before(atom_feat.shape), before(atom_feat.shape)],
        [
            pltpu.VMEM((3 * blocks, AUG, width), BF16),
            pltpu.VMEM((3, blocks, width), F32),
            pltpu.VMEM((blocks, AUG, width), BF16),
            pltpu.VMEM((2, 4, channels, width), BF16),
            pltpu.VMEM((2, filters, 4 * width, width), BF16),
        ],
        (2 * pairs * filters * channels, 8 << 20, 3 * pairs), 49 << 20,
    )
    asked = early[:, blocks * 3, :2].astype(jnp.int32).reshape(slots)
    sent = done.at[asked].get(mode="promise_in_bounds")
    replies = lax.all_to_all(
        sent.reshape(peers, 2 * channels, width), "tile", 0, 0, tiled=True
    ).reshape(slots, channels, width)

    pairs = tiles * reads * width * probes
    rows_shape = (tiles * reads, AUG, width)
    ready_shape = (READY, filters, probes // 128, width, 128)
    rows, goals, ready = plain(
        rows_kernel, (info, early, jnp.transpose(probe_pos, (1, 0, 2))), [SMEM, VMEM, VMEM],
        [VMEM, VMEM, pl.BlockSpec(memory_space=pl.ANY)],
        (
            jax.ShapeDtypeStruct(rows_shape, BF16),
            jax.ShapeDtypeStruct((tiles, probes // 128, AUG, 128), BF16),
            jax.ShapeDtypeStruct(ready_shape, BF16),
        ),
        [pltpu.VMEM(early.shape, F32), pltpu.VMEM(ready_shape, BF16), pltpu.SemaphoreType.DMA((READY,))],
        50 << 20, (1 << 30, 4 << 20, 1 << 20),
    )
    density, grad_probe, grad_mix, grad_read, back = plain(
        probe_kernel, (info, ready, rows, goals, replies, probe_target, probe_filter, mix_weight, readout.reshape(1, channels)),
        [SMEM, pl.BlockSpec(memory_space=pl.ANY)] + [VMEM] * 7, [VMEM] * 5,
        (
            jax.ShapeDtypeStruct((tiles, probes), F32),
            jax.ShapeDtypeStruct(probe_filter.shape, F32),
            jax.ShapeDtypeStruct(mix_weight.shape, F32),
            jax.ShapeDtypeStruct((1, channels), F32),
            jax.ShapeDtypeStruct(replies.shape, BF16),
        ),
        [pltpu.VMEM((filters, probes // 128, reads * width, 128), BF16) for _ in range(tiles)]
        + [
            pltpu.SemaphoreType.DMA((READY,)),
            pltpu.VMEM((probes // 128, filters * channels, 128), BF16),
            pltpu.VMEM((probes // 128, channels, 128), BF16),
            pltpu.VMEM((probes // 128, channels, 128), BF16),
            pltpu.VMEM((probes // 128, channels, 128), BF16),
            pltpu.VMEM((channels, 256), F32),
            pltpu.VMEM((filters * probes // 128, channels, 128), BF16),
            pltpu.VMEM(replies.shape, F32),
        ],
        50 << 20, (4 * pairs * filters * channels, 4 << 20, 3 * pairs),
    )
    returned = lax.all_to_all(
        back.reshape(peers, 2 * channels, width), "tile", 0, 0, tiled=True
    ).reshape(slots, channels, width)

    columns = 256
    part_shape = (devices, 24, width)
    parts = call(
        owner_kernel, (filters * channels // columns,), (asked,),
        (returned, slope, sums, grad_probe, grad_mix, grad_read),
        [whole(returned.shape), whole(slope.shape), pl.BlockSpec((blocks, columns, width), lambda j, *_: (0, j, 0)),
         whole(grad_probe.shape), whole(grad_mix.shape), whole((1, channels))],
        jax.ShapeDtypeStruct(part_shape, BF16), whole(part_shape),
        [pltpu.VMEM(slope.shape, F32), pltpu.VMEM(slope.shape, BF16)],
        (2 * blocks * width * channels * filters * channels, 8 << 20, 0), 49 << 20,
    )
    sums = reduced(parts)

    def filter_of(tiled):
        tall = tiled.reshape(channels // 8, filters, 8, channels)
        return jnp.transpose(tall, (0, 2, 1, 3)).reshape(channels, filters * channels).astype(F32)

    return (
        density,
        filter_of(sums[:, :8]),
        filter_of(sums[:, 8:16]),
        sums[: channels // 8, 16:].reshape(channels, channels).astype(F32),
        sums[channels // 8, 16].astype(F32),
    )


def solution(mesh):
    split2 = P(BOTH, None)
    split3d = P(BOTH, None, None)
    in_specs = (split3d, split3d, P(BOTH), split2, split3d, split2, split2, P(), P(), P(), P())
    out_specs = (split2, P(), P(), P(), P())
    return jax.shard_map(body, mesh=mesh, in_specs=in_specs, out_specs=out_specs, check_vma=False)
```

profile of v0, /device:TPU:1, one launch (start us, length us, event | category | flops | bytes accessed | tf_op | source)
XLA Modules:
  0.0 156.6 jit_solution(17390248232108194696)
XLA Ops:
  0.6 0.0 copy-start
  0.6 0.7 copy-done
  1.3 0.0 copy-start.1
  1.3 0.7 copy-done.1
  2.0 0.0 copy-start.2
  2.0 0.7 copy-done.2
  2.7 1.7 %requests.1 = (bf16[16,64,128]{2,1,0:T(8,128)(2,1)}, bf16[3,16,128]{2,1,0:T(8,128)(2,1)S(1)}, s32[3,16]{1,0:T(4,128)S(1)}) custom-call(s32[2,8]{1,0:T(2,128)S(1)} %copy-done.1, s32[16]{0:T(128)S(1)} %copy-done.2, bf16[3,16,128]{2,1,0:T(8,128)(2,1)S(1)} %bitcast.35), custom_call_target="tpu_custom_call" | custom-call | tf_op jit(solution)/shard_map/requests/pallas_call | solution.py:447
  4.4 8.6 %all-to-all-start = ((bf16[16,64,128]{2,1,0:T(8,128)(2,1)}), bf16[16,64,128]{2,1,0:T(8,128)(2,1)S(1)}, u32[]{:S(2)}, u32[]{:S(2)}) async-start(bf16[16,64,128]{2,1,0:T(8,128)(2,1)} %get-tuple-element.20), calls=%async_computation | async-start | bytes 524288 | tf_op jit(solution)/shard_map/all_to_all | solution.py:462
  13.0 2.1 %collective-permute-start = (bf16[16,128,128]{2,1,0:T(8,128)(2,1)}, bf16[16,128,128]{2,1,0:T(8,128)(2,1)S(1)}, u32[]{:S(2)}, u32[]{:S(2)}) collective-permute-start(bf16[16,128,128]{2,1,0:T(8,128)(2,1)} %own_ref.1), channel_id=1, source_target_pairs={{0,16},{16,32},{32,48},{48,64},{64,80},{80,96},{96,112},{112,0},{1... | collective-permute-start | bytes 1572872 | tf_op jit(solution)/shard_map/ppermute | solution.py:442
  15.0 0.0 collective-permute-start.1
  15.0 1.9 %collective-permute-start.3 = (bf16[3,16,128]{2,1,0:T(8,128)(2,1)S(1)}, bf16[3,16,128]{2,1,0:T(8,128)(2,1)S(1)}, u32[]{:S(2)}, u32[]{:S(2)}) collective-permute-start(bf16[3,16,128]{2,1,0:T(8,128)(2,1)S(1)} %get-tuple-element.24.own_pos), channel_id=1, source_target_pairs={{0,112},{16,0},{32,16},{48,32},{64,48},{80,64},{96,80},{112,96},{1... | collective-permute-start | bytes 36872 | tf_op jit(solution)/shard_map/ppermute | solution.py:461
  16.9 0.0 collective-permute-start.2
  16.9 3.5 %all-to-all-done.early_ref = bf16[16,64,128]{2,1,0:T(8,128)(2,1)S(1)} async-done(((bf16[16,64,128]{2,1,0:T(8,128)(2,1)}), bf16[16,64,128]{2,1,0:T(8,128)(2,1)S(1)}, u32[]{:S(2)}, u32[]{:S(2)}) %all-to-all-start) | async-done | bytes 262176 | tf_op jit(solution)/shard_map/all_to_all | solution.py:462
  20.5 0.1 reshape.72
  20.6 3.4 %collective-permute-done.3.hi_pos = bf16[3,16,128]{2,1,0:T(8,128)(2,1)S(1)} collective-permute-done((bf16[3,16,128]{2,1,0:T(8,128)(2,1)S(1)}, bf16[3,16,128]{2,1,0:T(8,128)(2,1)S(1)}, u32[]{:S(2)}, u32[]{:S(2)}) %collective-permute-start.3) | collective-permute-done | bytes 12320 | tf_op jit(solution)/shard_map/ppermute | solution.py:461
  24.0 0.0 collective-permute-done.2.lo_pos
  24.0 0.0 collective-permute-done.lo_ref
  24.0 0.0 collective-permute-done.1.hi_ref
  24.0 0.0 copy-start.3
  24.0 1.0 copy-done.3
  25.0 0.0 copy-start.4
  25.0 0.9 copy-done.4
  26.0 0.0 copy-start.9
  26.0 0.7 copy-done.9
  26.7 0.0 copy-start.7
  26.7 13.7 %shard_map.147 = (bf16[16,1024,128]{2,1,0:T(8,128)(2,1)}, f32[16,128,128]{2,1,0:T(8,128)S(1)}, bf16[16,128,128]{2,1,0:T(8,128)(2,1)S(1)}) custom-call(s32[4,16]{1,0:T(4,128)S(1)} %bitcast.37, bf16[16,128,128]{2,1,0:T(8,128)(2,1)S(1)} %collective-permute-done.lo_ref, bf16[16,128,128]{2,1,0:T(8,128)(2,1)S(1)} %copy-done.3, ...), custom_call_target="tpu_custom_call" | custom-call | flops 2147483648 | bytes 8388608 | tf_op jit(solution)/shard_map/pallas_call | solution.py:395
  40.4 0.0 copy-start.5
  40.4 0.0 copy-start.6
  40.4 0.0 copy-start.8
  40.4 0.0 copy-start.10
  40.4 1.7 %gather_fusion = bf16[32,128,128]{2,1,0:T(8,128)(2,1)} fusion(bf16[16,128,128]{2,1,0:T(8,128)(2,1)S(1)} %get-tuple-element.25, s32[1024]{0:T(1024)S(1)} %pad_clamp_fusion), kind=kCustom, calls=%fused_computation | custom fusion | bytes 2097280 | tf_op jit(solution)/shard_map/gather | solution.py:490
  42.1 6.9 %all-to-all-start.1 = ((bf16[16,256,128]{2,1,0:T(8,128)(2,1)}), bf16[16,256,128]{2,1,0:T(8,128)(2,1)S(1)}, u32[]{:S(2)}, u32[]{:S(2)}) async-start(bf16[16,256,128]{2,1,0:T(8,128)(2,1)} %bitcast.39), calls=%async_computation.1 | async-start | bytes 2097152 | tf_op jit(solution)/shard_map/all_to_all | solution.py:491
  49.0 0.0 copy-done.7
  49.0 3.5 %shard_map.146 = (bf16[16,16,128]{2,1,0:T(8,128)(2,1)S(1)}, bf16[2,4,16,128]{3,2,1,0:T(8,128)(2,1)S(1)}, bf16[5,8,4,128,128]{4,3,2,1,0:T(8,128)(2,1)}) custom-call(s32[3,16]{1,0:T(4,128)S(1)} %get-tuple-element.19.info_ref, bf16[16,64,128]{2,1,0:T(8,128)(2,1)S(1)} %all-to-all-done.early_ref, f32[3,2,512]{2,1,0:T(2,128)S(1)} %bitcast.36), custom_call_target="tpu_custom_call" | custom-call | flops 1073741824 | bytes 4194304 | tf_op jit(solution)/shard_map/pallas_call | solution.py:412
  52.6 12.7 %all-to-all-done.1 = bf16[16,256,128]{2,1,0:T(8,128)(2,1)S(1)} async-done(((bf16[16,256,128]{2,1,0:T(8,128)(2,1)}), bf16[16,256,128]{2,1,0:T(8,128)(2,1)S(1)}, u32[]{:S(2)}, u32[]{:S(2)}) %all-to-all-start.1) | async-done | bytes 1048608 | tf_op jit(solution)/shard_map/all_to_all | solution.py:491
  65.3 0.0 copy-done.5
  65.3 0.0 copy-done.6
  65.3 0.0 copy-done.8
  65.3 0.0 copy-done.10
  65.3 17.2 %shard_map.148 = (f32[2,512]{1,0:T(2,128)}, f32[128,1024]{1,0:T(8,128)S(1)}, f32[128,128]{1,0:T(8,128)S(1)}, f32[1,128]{1,0:T(1,128)S(1)}, bf16[32,128,128]{2,1,0:T(8,128)(2,1)}) custom-call(s32[3,16]{1,0:T(4,128)S(1)} %get-tuple-element.19.info_ref, bf16[5,8,4,128,128]{4,3,2,1,0:T(8,128)(2,1)} %get-tuple-element.21.ready_ref, ...), custom_call_target="tpu_custom_call" | custom-call | flops 4294967296 | bytes 4194304 | tf_op jit(solution)/shard_map/pallas_call | solution.py:412
  82.5 4.3 %all-to-all-start.2 = ((bf16[16,256,128]{2,1,0:T(8,128)(2,1)}), bf16[16,256,128]{2,1,0:T(8,128)(2,1)S(1)}, u32[]{:S(2)}, u32[]{:S(2)}) async-start(bf16[16,256,128]{2,1,0:T(8,128)(2,1)} %bitcast.7), calls=%async_computation.2 | async-start | bytes 2097152 | tf_op jit(solution)/shard_map/all_to_all | solution.py:532
  86.8 0.1 reshape.73.asked_ref
  86.9 15.1 %all-to-all-done.2 = bf16[16,256,128]{2,1,0:T(8,128)(2,1)S(1)} async-done(((bf16[16,256,128]{2,1,0:T(8,128)(2,1)}), bf16[16,256,128]{2,1,0:T(8,128)(2,1)S(1)}, u32[]{:S(2)}, u32[]{:S(2)}) %all-to-all-start.2) | async-done | bytes 1048608 | tf_op jit(solution)/shard_map/all_to_all | solution.py:532
  102.0 5.2 %shard_map.149 = bf16[128,24,128]{2,1,0:T(8,128)(2,1)S(1)} custom-call(s32[32]{0:T(128)S(1)} %reshape.73.asked_ref, bf16[32,128,128]{2,1,0:T(8,128)(2,1)S(1)} %bitcast.33, f32[16,128,128]{2,1,0:T(8,128)S(1)} %get-tuple-element.28.slope_ref, bf16[16,1024,128]{2,1,0:T(8,128)(2,1)} %get-tuple-element.29.sums_ref, f32[128,1024]{1,0:T(8,128)S(1)} %get-tuple-element.30.probe_ref, ...), custom_call_target="tpu_custom_call" | custom-call | flops 536870912 | bytes 8388608 | tf_op jit(solution)/shard_map/pallas_call | solution.py:395
  107.1 26.6 %all_to_all.25.parts_ref = bf16[128,24,128]{2,1,0:T(8,128)(2,1)S(1)} all-to-all(bf16[128,24,128]{2,1,0:T(8,128)(2,1)S(1)} %shard_map.149), channel_id=1, replica_groups=mesh['space'=8,'tile'=16] {'space','tile'}, dimensions={0} | all-to-all | bytes 1572864 | tf_op jit(solution)/shard_map/all_to_all | solution.py:420
  133.7 0.2 spread.1
  133.9 20.4 %all_to_all.26 = bf16[128,24,128]{2,1,0:T(8,128)(2,1)S(1)} all-to-all(bf16[128,24,128]{2,1,0:T(8,128)(2,1)S(1)} %spread.1), channel_id=1, replica_groups=mesh['space'=8,'tile'=16] {'space','tile'}, dimensions={0} | all-to-all | bytes 1572864 | tf_op jit(solution)/shard_map/all_to_all | solution.py:426
  154.4 1.1 convert_bitcast_fusion
  155.5 0.5 fusion.2
  156.0 0.6 fusion
  (5 shorter events, 0.1 us)
Async XLA Ops:
  0.6 0.7 copy-start
  1.3 0.7 copy-start.1
  2.0 0.7 copy-start.2
  4.4 16.1 %all-to-all-start = ((bf16[16,64,128]{2,1,0:T(8,128)(2,1)}), bf16[16,64,128]{2,1,0:T(8,128)(2,1)S(1)}, u32[]{:S(2)}, u32[]{:S(2)}) async-start(bf16[16,64,128]{2,1,0:T(8,128)(2,1)} %get-tuple-element.20), calls=%async_computation | async-start | bytes 524288 | tf_op jit(solution)/shard_map/all_to_all | solution.py:462
  13.0 11.0 %collective-permute-start = (bf16[16,128,128]{2,1,0:T(8,128)(2,1)}, bf16[16,128,128]{2,1,0:T(8,128)(2,1)S(1)}, u32[]{:S(2)}, u32[]{:S(2)}) collective-permute-start(bf16[16,128,128]{2,1,0:T(8,128)(2,1)} %own_ref.1), channel_id=1, source_target_pairs={{0,16},{16,32},{32,48},{48,64},{64,80},{80,96},{96,112},{112,0},{1... | collective-permute-start | bytes 1572872 | tf_op jit(solution)/shard_map/ppermute | solution.py:442
  15.0 9.0 %collective-permute-start.1 = (bf16[16,128,128]{2,1,0:T(8,128)(2,1)}, bf16[16,128,128]{2,1,0:T(8,128)(2,1)S(1)}, u32[]{:S(2)}, u32[]{:S(2)}) collective-permute-start(bf16[16,128,128]{2,1,0:T(8,128)(2,1)} %own_ref.1), channel_id=1, source_target_pairs={{0,112},{16,0},{32,16},{48,32},{64,48},{80,64},{96,80},{112,96},{1... | collective-permute-start | bytes 1572872 | tf_op jit(solution)/shard_map/ppermute | solution.py:443
  15.0 8.9 %collective-permute-start.3 = (bf16[3,16,128]{2,1,0:T(8,128)(2,1)S(1)}, bf16[3,16,128]{2,1,0:T(8,128)(2,1)S(1)}, u32[]{:S(2)}, u32[]{:S(2)}) collective-permute-start(bf16[3,16,128]{2,1,0:T(8,128)(2,1)S(1)} %get-tuple-element.24.own_pos), channel_id=1, source_target_pairs={{0,112},{16,0},{32,16},{48,32},{64,48},{80,64},{96,80},{112,96},{1... | collective-permute-start | bytes 36872 | tf_op jit(solution)/shard_map/ppermute | solution.py:461
  16.9 7.1 %collective-permute-start.2 = (bf16[3,16,128]{2,1,0:T(8,128)(2,1)S(1)}, bf16[3,16,128]{2,1,0:T(8,128)(2,1)S(1)}, u32[]{:S(2)}, u32[]{:S(2)}) collective-permute-start(bf16[3,16,128]{2,1,0:T(8,128)(2,1)S(1)} %get-tuple-element.24.own_pos), channel_id=1, source_target_pairs={{0,16},{16,32},{32,48},{48,64},{64,80},{80,96},{96,112},{112,0},{1... | collective-permute-start | bytes 36872 | tf_op jit(solution)/shard_map/ppermute | solution.py:460
  24.0 1.0 copy-start.3
  25.0 0.9 copy-start.4
  26.0 0.7 copy-start.9
  26.7 22.4 %copy-start.7 = (f32[2,3,512]{2,0,1:T(2,128)S(1)}, f32[2,3,512]{2,0,1:T(2,128)}, u32[]{:S(2)}) copy-start(f32[2,3,512]{2,0,1:T(2,128)} %param.15) | copy-start | bytes 36868
  40.4 24.9 %copy-start.5 = (bf16[128,1024]{1,0:T(8,128)(2,1)S(1)}, bf16[128,1024]{1,0:T(8,128)(2,1)}, u32[]{:S(2)}) copy-start(bf16[128,1024]{1,0:T(8,128)(2,1)} %weight_ref.3) | copy-start | bytes 786436
  40.4 24.9 %copy-start.6 = (bf16[128,128]{1,0:T(8,128)(2,1)S(1)}, bf16[128,128]{1,0:T(8,128)(2,1)}, u32[]{:S(2)}) copy-start(bf16[128,128]{1,0:T(8,128)(2,1)} %mix_ref.1) | copy-start | bytes 98308
  40.4 24.9 %copy-start.8 = (f32[2,512]{1,0:T(2,128)S(1)}, f32[2,512]{1,0:T(2,128)}, u32[]{:S(2)}) copy-start(f32[2,512]{1,0:T(2,128)} %goal_ref.1) | copy-start | bytes 12292
  40.4 24.9 %copy-start.10 = (f32[128]{0:T(128)S(1)}, f32[128]{0:T(128)}, u32[]{:S(2)}) copy-start(f32[128]{0:T(128)} %param.21) | copy-start | bytes 1540
  42.1 23.2 %all-to-all-start.1 = ((bf16[16,256,128]{2,1,0:T(8,128)(2,1)}), bf16[16,256,128]{2,1,0:T(8,128)(2,1)S(1)}, u32[]{:S(2)}, u32[]{:S(2)}) async-start(bf16[16,256,128]{2,1,0:T(8,128)(2,1)} %bitcast.39), calls=%async_computation.1 | async-start | bytes 2097152 | tf_op jit(solution)/shard_map/all_to_all | solution.py:491
  82.5 19.4 %all-to-all-start.2 = ((bf16[16,256,128]{2,1,0:T(8,128)(2,1)}), bf16[16,256,128]{2,1,0:T(8,128)(2,1)S(1)}, u32[]{:S(2)}, u32[]{:S(2)}) async-start(bf16[16,256,128]{2,1,0:T(8,128)(2,1)} %bitcast.7), calls=%async_computation.2 | async-start | bytes 2097152 | tf_op jit(solution)/shard_map/all_to_all | solution.py:532
where the time goes:
time: 157 us
  blocking collectives  47 us (30%)
  Pallas kernels  41.5 us (26%)
  waiting for transfers between devices  34.7 us (22%)
  starting transfers between devices  23.7 us (15%)
  local copies, waits for them, and re-layouts  6.59 us (4%)
  other arithmetic  2.29 us (1%)
    all_to_all x1, blocking collectives, reduced(): sent = lax.all_to_all(chunks, BOTH, 0, 0, tiled=True)  26.6 us
    pallas_call x2, Pallas kernels, plain(): pl.pallas_call(kernel, in_specs=in_specs, out_specs=out_specs, out_shape=...  20.8 us
    all_to_all x1, blocking collectives, reduced(): return lax.all_to_all(totals, BOTH, 0, 0, tiled=True)  20.4 us
    pallas_call x2, Pallas kernels, call(): pl.pallas_call(kernel, grid_spec=pltpu.PrefetchScalarGridSpec(num_scalar_...  18.9 us
    all_to_all x1, waiting for transfers between devices, body(): lax.all_to_all(back.reshape(peers, 2 * channels, width), 'tile', 0, 0, ti...  15.1 us
    all_to_all x1, waiting for transfers between devices, body(): lax.all_to_all(sent.reshape(peers, 2 * channels, width), 'tile', 0, 0, ti...  12.7 us
    all_to_all x1, starting transfers between devices, body(): early = lax.all_to_all(early, 'tile', 0, 0, tiled=True)  8.6 us
    all_to_all x1, starting transfers between devices, body(): lax.all_to_all(sent.reshape(peers, 2 * channels, width), 'tile', 0, 0, ti...  6.94 us
  transfers between devices with their start and end apart: 7, of which 4 were waited for; matrix products, arithmetic and copies ran while one was open for 0% of the time, Pallas kernels for 2%

commit v1 on v0

--- a/solution.py
+++ b/solution.py
@@ -18,7 +18,7 @@
 SPREAD = 0.75
 SOFT = 0.01
 AUG = 16
-READY = 5
+READY = (0, 1, 2, 8, 9, 10, 11, 12, 13, 14, 15)
 MARK = 32.0
 
 
@@ -125,8 +125,8 @@
         early_ref[t, 3 * blocks :, :] = note.astype(F32).astype(BF16)
 
 
-def atom_kernel(peers, nbr_ref, lo_ref, own_ref, hi_ref, lo_pos, own_pos, hi_pos, weight_ref,
-                sums_ref, slope_ref, done_ref, rows, masks, goals, feat, kern):
+def atom_kernel(peers, nbr_ref, lo_ref, own_hbm, hi_ref, lo_pos, own_pos, hi_pos, weight_hbm,
+                sums_ref, slope_ref, done_ref, own_ref, weight_ref, landed, rows, masks, goals, feat, kern, both):
     b = pl.program_id(0)
     blocks, channels, width = own_ref.shape
     nbrs = feat.shape[1]
@@ -135,6 +135,12 @@
 
     @pl.when(b == 0)
     def _():
+        fetches = [
+            pltpu.make_async_copy(own_hbm, own_ref, landed.at[0]),
+            pltpu.make_async_copy(weight_hbm, weight_ref, landed.at[1]),
+        ]
+        for copy in fetches:
+            copy.start()
         for s, pos in enumerate((lo_pos, own_pos, hi_pos)):
             wide = [pos[c].astype(F32) for c in range(3)]
             there = wide[0] < MARK
@@ -145,6 +151,8 @@
                 rows[s * blocks + i] = source_rows(x, y, z)
                 if s == 1:
                     goals[i] = target_rows(x, y, z)
+        for copy in fetches:
+            copy.wait()
 
     def pick(slot, k, feats, s, index):
         mask = jnp.broadcast_to(masks[s, pl.ds(index, 1), :], (channels, width)).astype(BF16)
@@ -164,10 +172,13 @@
         part = dot(feats, kerns, (1, 0))
         for i in range(2):
             piece = part[:, i * width : (i + 1) * width] * decay(r + i)
-            sums_ref[0, (r + i) * channels : (r + i + 1) * channels, :] = piece.astype(BF16)
-
-    def last(at):
-        sums = sums_ref[0]
+            piece = piece.astype(BF16)
+            lines = slice((r + i) * channels, (r + i + 1) * channels)
+            sums_ref[0, lines, :] = piece
+            both[slot, lines, :] = piece
+
+    def last(slot, at):
+        sums = both[slot]
         message = dot(weight_ref[...], sums, (1, 0))
         mask = masks[1, pl.ds(at, 1), :]
         gate = sigmoid(message)
@@ -192,7 +203,8 @@
         for k in range(nbrs):
             prepare(slot, k, sides[k] * blocks + index[k])
             finish(1 - slot, 2 * k)
-        last(jnp.maximum(b - 1, 0))
+            if k == 1:
+                last(slot, jnp.clip(b - 2, 0, blocks - 1))
 
     @pl.when(b % 2 == 0)
     def _():
@@ -226,11 +238,11 @@
     def leave(k):
         return pltpu.make_async_copy(held.at[k], kern_ref.at[k], left.at[k])
 
-    for k in range(held.shape[0]):
+    for k, block in enumerate(READY):
         def store(at, r, value):
             held[k, r, at] = value
 
-        radial_block(rows_ref[k], goals_ref, 0, scale, held.shape[1], store)
+        radial_block(rows_ref[block], goals_ref, block // reads, scale, held.shape[1], store)
         leave(k).start()
     for k in range(held.shape[0]):
         leave(k).wait()
@@ -248,7 +260,10 @@
     kerns = (first, second)
 
     def fetch(k):
-        return pltpu.make_async_copy(ready_ref.at[k], first.at[:, :, k * width : (k + 1) * width, :], arrived.at[k])
+        t, at = divmod(READY[k], reads)
+        return pltpu.make_async_copy(
+            ready_ref.at[k], kerns[t].at[:, :, at * width : (at + 1) * width, :], arrived.at[k]
+        )
 
     for k in range(ready):
         fetch(k).start()
@@ -327,17 +342,15 @@
                 slot = info_ref[0, t * reads + k + i]
                 total[slot] += part[:, i * width : (i + 1) * width]
 
-    @pl.loop(0, reads)
-    def _(k):
-        radial(1, k)
-
-    @pl.loop(ready, reads)
-    def _(k):
-        radial(0, k)
-
-    for k in range(ready):
-        fetch(k).wait()
+    for t in reversed(range(tiles)):
+        @pl.loop(sum(block // reads == t for block in READY), reads)
+        def _(k):
+            radial(t, k)
+
     for t in range(tiles):
+        for k, block in enumerate(READY):
+            if block // reads == t:
+                fetch(k).wait()
         forward(t)
         middle(t)
         backward(t)
@@ -406,6 +419,11 @@
 
 SMEM = pl.BlockSpec(memory_space=pltpu.SMEM)
 VMEM = pl.BlockSpec(memory_space=pltpu.VMEM)
+HBM = pl.BlockSpec(memory_space=pltpu.HBM)
+
+
+def in_hbm(value):
+    return pltpu.with_memory_space_constraint(value, pltpu.HBM)
 
 
 def plain(kernel, ins, in_specs, out_specs, outs, scratch, limit, cost=None):
@@ -456,33 +474,40 @@
         scratch_shapes=[pltpu.SMEM((slots,), jnp.int32)],
         name="requests",
         compiler_params=pltpu.CompilerParams(vmem_limit_bytes=4 << 20),
-    )(tile_blocks, atom_counts, where)
+    )(in_hbm(tile_blocks), in_hbm(atom_counts), in_hbm(where))
     pos_lo = lax.ppermute(marked, "space", up)
     pos_hi = lax.ppermute(marked, "space", down)
     early = lax.all_to_all(early, "tile", 0, 0, tiled=True)
 
     pairs = blocks * 4 * width * width
 
-    def before(shape):
-        return pl.BlockSpec((1, *shape[1:]), lambda b, *_: (jnp.maximum(b - 1, 0),) + (0,) * (len(shape) - 1))
+    def before(shape, steps):
+        def index(b, *_):
+            return (jnp.clip(b - steps, 0, blocks - 1),) + (0,) * (len(shape) - 1)
+
+        return pl.BlockSpec((1, *shape[1:]), index)
 
     sums_shape = (blocks, filters * channels, width)
     sums, slope, done = call(
-        functools.partial(atom_kernel, peers), (blocks + 1,), (atom_nbrs.T,),
-        (feat_lo, atom_feat, feat_hi, pos_lo, marked, pos_hi, atom_filter),
-        [whole(atom_feat.shape)] * 3 + [whole(marked.shape)] * 3 + [whole(atom_filter.shape)],
+        functools.partial(atom_kernel, peers), (blocks + 2,), (in_hbm(atom_nbrs.T),),
+        (feat_lo, in_hbm(atom_feat), feat_hi, pos_lo, marked, pos_hi, in_hbm(atom_filter)),
+        [whole(atom_feat.shape), HBM, whole(atom_feat.shape)] + [whole(marked.shape)] * 3 + [HBM],
         (
             jax.ShapeDtypeStruct(sums_shape, BF16),
             jax.ShapeDtypeStruct(atom_feat.shape, F32),
             jax.ShapeDtypeStruct(atom_feat.shape, BF16),
         ),
-        [before(sums_shape), before(atom_feat.shape), before(atom_feat.shape)],
+        [before(sums_shape, 1), before(atom_feat.shape, 2), before(atom_feat.shape, 2)],
         [
+            pltpu.VMEM(atom_feat.shape, BF16),
+            pltpu.VMEM(atom_filter.shape, BF16),
+            pltpu.SemaphoreType.DMA((2,)),
             pltpu.VMEM((3 * blocks, AUG, width), BF16),
             pltpu.VMEM((3, blocks, width), F32),
             pltpu.VMEM((blocks, AUG, width), BF16),
             pltpu.VMEM((2, 4, channels, width), BF16),
             pltpu.VMEM((2, filters, 4 * width, width), BF16),
+            pltpu.VMEM((2, filters * channels, width), BF16),
         ],
         (2 * pairs * filters * channels, 8 << 20, 3 * pairs), 49 << 20,
     )
@@ -494,7 +519,7 @@
 
     pairs = tiles * reads * width * probes
     rows_shape = (tiles * reads, AUG, width)
-    ready_shape = (READY, filters, probes // 128, width, 128)
+    ready_shape = (len(READY), filters, probes // 128, width, 128)
     rows, goals, ready = plain(
         rows_kernel, (info, early, jnp.transpose(probe_pos, (1, 0, 2))), [SMEM, VMEM, VMEM],
         [VMEM, VMEM, pl.BlockSpec(memory_space=pl.ANY)],
@@ -503,7 +528,7 @@
             jax.ShapeDtypeStruct((tiles, probes // 128, AUG, 128), BF16),
             jax.ShapeDtypeStruct(ready_shape, BF16),
         ),
-        [pltpu.VMEM(early.shape, F32), pltpu.VMEM(ready_shape, BF16), pltpu.SemaphoreType.DMA((READY,))],
+        [pltpu.VMEM(early.shape, F32), pltpu.VMEM(ready_shape, BF16), pltpu.SemaphoreType.DMA((len(READY),))],
         50 << 20, (1 << 30, 4 << 20, 1 << 20),
     )
     density, grad_probe, grad_mix, grad_read, back = plain(
@@ -518,7 +543,7 @@
         ),
         [pltpu.VMEM((filters, probes // 128, reads * width, 128), BF16) for _ in range(tiles)]
         + [
-            pltpu.SemaphoreType.DMA((READY,)),
+            pltpu.SemaphoreType.DMA((len(READY),)),
             pltpu.VMEM((probes // 128, filters * channels, 128), BF16),
             pltpu.VMEM((probes // 128, channels, 128), BF16),
             pltpu.VMEM((probes // 128, channels, 128), BF16),

time: 157 us -> 151 us (0.962)
  local copies, waits for them, and re-layouts: 6.59 us -> 1.89 us
  waiting for transfers between devices: 34.7 us -> 32.7 us
    unnamed x22 -> x10, local copies, waits for them, and re-layouts: 4.72 us -> 0.02 us
    all_to_all x1, waiting for transfers between devices: 12.7 us -> 10.7 us  [body(): lax.all_to_all(sent.reshape(peers, 2 * channels, width), 'tile', 0, 0, ti...]
  transfers between devices with their start and end apart: 7 -> 7, of which waited for: 4 -> 4; matrix products, arithmetic and copies ran while one was open for 0% -> 0% of each run, Pallas kernels for 2% -> 4%
where the time goes in v1:
time: 151 us; the launch traced here: 150 us
  blocking collectives  47 us (31%)
  Pallas kernels  41.8 us (28%)
  waiting for transfers between devices  32.7 us (22%)
  starting transfers between devices  23.7 us (16%)
  other arithmetic  2.29 us (2%)
  local copies, waits for them, and re-layouts  1.89 us (1%)
    all_to_all x1, blocking collectives, reduced(): sent = lax.all_to_all(chunks, BOTH, 0, 0, tiled=True)  26.6 us
    all_to_all x1, blocking collectives, reduced(): return lax.all_to_all(totals, BOTH, 0, 0, tiled=True)  20.4 us
    pallas_call x2, Pallas kernels, plain(): pl.pallas_call(kernel, in_specs=in_specs, out_specs=out_specs, out_shape=...  20.4 us
    pallas_call x2, Pallas kernels, call(): pl.pallas_call(kernel, grid_spec=pltpu.PrefetchScalarGridSpec(num_scalar_...  19.3 us
    all_to_all x1, waiting for transfers between devices, body(): lax.all_to_all(back.reshape(peers, 2 * channels, width), 'tile', 0, 0, ti...  15.1 us
    all_to_all x1, waiting for transfers between devices, body(): lax.all_to_all(sent.reshape(peers, 2 * channels, width), 'tile', 0, 0, ti...  10.7 us
    all_to_all x1, starting transfers between devices, body(): early = lax.all_to_all(early, 'tile', 0, 0, tiled=True)  8.6 us
    all_to_all x1, starting transfers between devices, body(): lax.all_to_all(sent.reshape(peers, 2 * channels, width), 'tile', 0, 0, ti...  6.94 us
  transfers between devices with their start and end apart: 7, of which 4 were waited for; matrix products, arithmetic and copies ran while one was open for 0% of the time, Pallas kernels for 4%

profile of v1, /device:TPU:1, one launch (start us, length us, event | category | flops | bytes accessed | tf_op | source)
XLA Modules:
  0.0 150.3 jit_solution(9803244838472281602)
XLA Ops:
  0.6 0.0 copy-start.2
  0.6 0.0 copy-start.4
  0.7 0.0 copy-start.1
  0.7 0.0 copy-start
  0.7 0.0 copy-start.3
  0.7 2.0 %requests.1 = (bf16[16,64,128]{2,1,0:T(8,128)(2,1)}, bf16[3,16,128]{2,1,0:T(8,128)(2,1)S(1)}, s32[3,16]{1,0:T(4,128)S(1)}) custom-call(s32[2,8]{1,0:T(2,128)} %reads_ref.1, s32[16]{0:T(128)} %counts_ref.1, bf16[3,16,128]{2,1,0:T(8,128)(2,1)} %bitcast.41), custom_call_target="tpu_custom_call" | custom-call | tf_op jit(solution)/shard_map/requests/pallas_call | solution.py:465
  2.6 8.6 %all-to-all-start = ((bf16[16,64,128]{2,1,0:T(8,128)(2,1)}), bf16[16,64,128]{2,1,0:T(8,128)(2,1)S(1)}, u32[]{:S(2)}, u32[]{:S(2)}) async-start(bf16[16,64,128]{2,1,0:T(8,128)(2,1)} %get-tuple-element.20), calls=%async_computation | async-start | bytes 524288 | tf_op jit(solution)/shard_map/all_to_all | solution.py:480
  11.3 2.1 %collective-permute-start = (bf16[16,128,128]{2,1,0:T(8,128)(2,1)}, bf16[16,128,128]{2,1,0:T(8,128)(2,1)S(1)}, u32[]{:S(2)}, u32[]{:S(2)}) collective-permute-start(bf16[16,128,128]{2,1,0:T(8,128)(2,1)} %own_hbm.1), channel_id=1, source_target_pairs={{0,16},{16,32},{32,48},{48,64},{64,80},{80,96},{96,112},{112,0},{1... | collective-permute-start | bytes 1572872 | tf_op jit(solution)/shard_map/ppermute | solution.py:460
  13.3 0.0 collective-permute-start.1
  13.3 1.9 %collective-permute-start.3 = (bf16[3,16,128]{2,1,0:T(8,128)(2,1)S(1)}, bf16[3,16,128]{2,1,0:T(8,128)(2,1)S(1)}, u32[]{:S(2)}, u32[]{:S(2)}) collective-permute-start(bf16[3,16,128]{2,1,0:T(8,128)(2,1)S(1)} %get-tuple-element.24.own_pos), channel_id=1, source_target_pairs={{0,112},{16,0},{32,16},{48,32},{64,48},{80,64},{96,80},{112,96},{1... | collective-permute-start | bytes 36872 | tf_op jit(solution)/shard_map/ppermute | solution.py:479
  15.2 0.0 collective-permute-start.2
  15.2 3.5 %all-to-all-done.early_ref = bf16[16,64,128]{2,1,0:T(8,128)(2,1)S(1)} async-done(((bf16[16,64,128]{2,1,0:T(8,128)(2,1)}), bf16[16,64,128]{2,1,0:T(8,128)(2,1)S(1)}, u32[]{:S(2)}, u32[]{:S(2)}) %all-to-all-start) | async-done | bytes 262176 | tf_op jit(solution)/shard_map/all_to_all | solution.py:480
  18.7 0.1 reshape.72
  18.9 3.4 %collective-permute-done.3.hi_pos = bf16[3,16,128]{2,1,0:T(8,128)(2,1)S(1)} collective-permute-done((bf16[3,16,128]{2,1,0:T(8,128)(2,1)S(1)}, bf16[3,16,128]{2,1,0:T(8,128)(2,1)S(1)}, u32[]{:S(2)}, u32[]{:S(2)}) %collective-permute-start.3) | collective-permute-done | bytes 12320 | tf_op jit(solution)/shard_map/ppermute | solution.py:479
  22.3 0.0 collective-permute-done.2.lo_pos
  22.3 0.0 collective-permute-done.lo_ref
  22.3 0.0 collective-permute-done.1.hi_ref
  22.3 14.1 %shard_map.147 = (bf16[16,1024,128]{2,1,0:T(8,128)(2,1)}, f32[16,128,128]{2,1,0:T(8,128)S(1)}, bf16[16,128,128]{2,1,0:T(8,128)(2,1)S(1)}) custom-call(s32[4,16]{1,0:T(4,128)} %bitcast.42, bf16[16,128,128]{2,1,0:T(8,128)(2,1)S(1)} %collective-permute-done.lo_ref, bf16[16,128,128]{2,1,0:T(8,128)(2,1)} %own_hbm.1, ...), custom_call_target="tpu_custom_call" | custom-call | flops 2147483648 | bytes 8388608 | tf_op jit(solution)/shard_map/pallas_call | solution.py:408
  36.4 1.7 %gather_fusion = bf16[32,128,128]{2,1,0:T(8,128)(2,1)} fusion(bf16[16,128,128]{2,1,0:T(8,128)(2,1)S(1)} %get-tuple-element.25, s32[1024]{0:T(1024)S(1)} %pad_clamp_fusion), kind=kCustom, calls=%fused_computation | custom fusion | bytes 2097280 | tf_op jit(solution)/shard_map/gather | solution.py:515
  38.1 6.9 %all-to-all-start.1 = ((bf16[16,256,128]{2,1,0:T(8,128)(2,1)}), bf16[16,256,128]{2,1,0:T(8,128)(2,1)S(1)}, u32[]{:S(2)}, u32[]{:S(2)}) async-start(bf16[16,256,128]{2,1,0:T(8,128)(2,1)} %bitcast.37), calls=%async_computation.1 | async-start | bytes 2097152 | tf_op jit(solution)/shard_map/all_to_all | solution.py:516
  45.0 0.0 copy-done.2
  45.0 5.5 %shard_map.146 = (bf16[16,16,128]{2,1,0:T(8,128)(2,1)S(1)}, bf16[2,4,16,128]{3,2,1,0:T(8,128)(2,1)S(1)}, bf16[11,8,4,128,128]{4,3,2,1,0:T(8,128)(2,1)}) custom-call(s32[3,16]{1,0:T(4,128)S(1)} %get-tuple-element.19.info_ref, bf16[16,64,128]{2,1,0:T(8,128)(2,1)S(1)} %all-to-all-done.early_ref, f32[3,2,512]{2,1,0:T(2,128)S(1)} %bitcast.35), custom_call_target="tpu_custom_call" | custom-call | flops 1073741824 | bytes 4194304 | tf_op jit(solution)/shard_map/pallas_call | solution.py:430
  50.6 10.7 %all-to-all-done.1 = bf16[16,256,128]{2,1,0:T(8,128)(2,1)S(1)} async-done(((bf16[16,256,128]{2,1,0:T(8,128)(2,1)}), bf16[16,256,128]{2,1,0:T(8,128)(2,1)S(1)}, u32[]{:S(2)}, u32[]{:S(2)}) %all-to-all-start.1) | async-done | bytes 1048608 | tf_op jit(solution)/shard_map/all_to_all | solution.py:516
  61.3 0.0 copy-done.4
  61.3 0.0 copy-done.1
  61.3 0.0 copy-done
  61.3 0.0 copy-done.3
  61.3 14.9 %shard_map.148 = (f32[2,512]{1,0:T(2,128)}, f32[128,1024]{1,0:T(8,128)S(1)}, f32[128,128]{1,0:T(8,128)S(1)}, f32[1,128]{1,0:T(1,128)S(1)}, bf16[32,128,128]{2,1,0:T(8,128)(2,1)}) custom-call(s32[3,16]{1,0:T(4,128)S(1)} %get-tuple-element.19.info_ref, bf16[11,8,4,128,128]{4,3,2,1,0:T(8,128)(2,1)} %get-tuple-element.21.ready_ref, ...), custom_call_target="tpu_custom_call" | custom-call | flops 4294967296 | bytes 4194304 | tf_op jit(solution)/shard_map/pallas_call | solution.py:430
  76.1 4.3 %all-to-all-start.2 = ((bf16[16,256,128]{2,1,0:T(8,128)(2,1)}), bf16[16,256,128]{2,1,0:T(8,128)(2,1)S(1)}, u32[]{:S(2)}, u32[]{:S(2)}) async-start(bf16[16,256,128]{2,1,0:T(8,128)(2,1)} %bitcast.7), calls=%async_computation.2 | async-start | bytes 2097152 | tf_op jit(solution)/shard_map/all_to_all | solution.py:557
  80.4 0.1 reshape.73.asked_ref
  80.5 15.1 %all-to-all-done.2 = bf16[16,256,128]{2,1,0:T(8,128)(2,1)S(1)} async-done(((bf16[16,256,128]{2,1,0:T(8,128)(2,1)}), bf16[16,256,128]{2,1,0:T(8,128)(2,1)S(1)}, u32[]{:S(2)}, u32[]{:S(2)}) %all-to-all-start.2) | async-done | bytes 1048608 | tf_op jit(solution)/shard_map/all_to_all | solution.py:557
  95.6 5.1 %shard_map.149 = bf16[128,24,128]{2,1,0:T(8,128)(2,1)S(1)} custom-call(s32[32]{0:T(128)S(1)} %reshape.73.asked_ref, bf16[32,128,128]{2,1,0:T(8,128)(2,1)S(1)} %bitcast.33, f32[16,128,128]{2,1,0:T(8,128)S(1)} %get-tuple-element.28.slope_ref, bf16[16,1024,128]{2,1,0:T(8,128)(2,1)} %get-tuple-element.29.sums_ref, f32[128,1024]{1,0:T(8,128)S(1)} %get-tuple-element.30.probe_ref, ...), custom_call_target="tpu_custom_call" | custom-call | flops 536870912 | bytes 8388608 | tf_op jit(solution)/shard_map/pallas_call | solution.py:408
  100.7 26.6 %all_to_all.25.parts_ref = bf16[128,24,128]{2,1,0:T(8,128)(2,1)S(1)} all-to-all(bf16[128,24,128]{2,1,0:T(8,128)(2,1)S(1)} %shard_map.149), channel_id=1, replica_groups=mesh['space'=8,'tile'=16] {'space','tile'}, dimensions={0} | all-to-all | bytes 1572864 | tf_op jit(solution)/shard_map/all_to_all | solution.py:438
  127.4 0.2 spread.1
  127.5 20.4 %all_to_all.26 = bf16[128,24,128]{2,1,0:T(8,128)(2,1)S(1)} all-to-all(bf16[128,24,128]{2,1,0:T(8,128)(2,1)S(1)} %spread.1), channel_id=1, replica_groups=mesh['space'=8,'tile'=16] {'space','tile'}, dimensions={0} | all-to-all | bytes 1572864 | tf_op jit(solution)/shard_map/all_to_all | solution.py:444
  148.0 1.1 convert_bitcast_fusion
  149.1 0.5 fusion.2
  149.6 0.6 fusion
  (5 shorter events, 0.1 us)
Async XLA Ops:
  0.6 44.4 %copy-start.2 = (f32[2,3,512]{2,0,1:T(2,128)S(1)}, f32[2,3,512]{2,0,1:T(2,128)}, u32[]{:S(2)}) copy-start(f32[2,3,512]{2,0,1:T(2,128)} %param.15) | copy-start | bytes 36868
  0.6 60.6 %copy-start.4 = (f32[128]{0:T(128)S(1)}, f32[128]{0:T(128)}, u32[]{:S(2)}) copy-start(f32[128]{0:T(128)} %param.21) | copy-start | bytes 1540
  0.7 60.6 %copy-start.1 = (bf16[128,128]{1,0:T(8,128)(2,1)S(1)}, bf16[128,128]{1,0:T(8,128)(2,1)}, u32[]{:S(2)}) copy-start(bf16[128,128]{1,0:T(8,128)(2,1)} %mix_ref.1) | copy-start | bytes 98308
  0.7 60.6 %copy-start = (bf16[128,1024]{1,0:T(8,128)(2,1)S(1)}, bf16[128,1024]{1,0:T(8,128)(2,1)}, u32[]{:S(2)}) copy-start(bf16[128,1024]{1,0:T(8,128)(2,1)} %weight_ref.1) | copy-start | bytes 786436
  0.7 60.6 %copy-start.3 = (f32[2,512]{1,0:T(2,128)S(1)}, f32[2,512]{1,0:T(2,128)}, u32[]{:S(2)}) copy-start(f32[2,512]{1,0:T(2,128)} %goal_ref.1) | copy-start | bytes 12292
  2.6 16.1 %all-to-all-start = ((bf16[16,64,128]{2,1,0:T(8,128)(2,1)}), bf16[16,64,128]{2,1,0:T(8,128)(2,1)S(1)}, u32[]{:S(2)}, u32[]{:S(2)}) async-start(bf16[16,64,128]{2,1,0:T(8,128)(2,1)} %get-tuple-element.20), calls=%async_computation | async-start | bytes 524288 | tf_op jit(solution)/shard_map/all_to_all | solution.py:480
  11.3 11.0 %collective-permute-start = (bf16[16,128,128]{2,1,0:T(8,128)(2,1)}, bf16[16,128,128]{2,1,0:T(8,128)(2,1)S(1)}, u32[]{:S(2)}, u32[]{:S(2)}) collective-permute-start(bf16[16,128,128]{2,1,0:T(8,128)(2,1)} %own_hbm.1), channel_id=1, source_target_pairs={{0,16},{16,32},{32,48},{48,64},{64,80},{80,96},{96,112},{112,0},{1... | collective-permute-start | bytes 1572872 | tf_op jit(solution)/shard_map/ppermute | solution.py:460
  13.3 9.0 %collective-permute-start.1 = (bf16[16,128,128]{2,1,0:T(8,128)(2,1)}, bf16[16,128,128]{2,1,0:T(8,128)(2,1)S(1)}, u32[]{:S(2)}, u32[]{:S(2)}) collective-permute-start(bf16[16,128,128]{2,1,0:T(8,128)(2,1)} %own_hbm.1), channel_id=1, source_target_pairs={{0,112},{16,0},{32,16},{48,32},{64,48},{80,64},{96,80},{112,96},{1... | collective-permute-start | bytes 1572872 | tf_op jit(solution)/shard_map/ppermute | solution.py:461
  13.3 8.9 %collective-permute-start.3 = (bf16[3,16,128]{2,1,0:T(8,128)(2,1)S(1)}, bf16[3,16,128]{2,1,0:T(8,128)(2,1)S(1)}, u32[]{:S(2)}, u32[]{:S(2)}) collective-permute-start(bf16[3,16,128]{2,1,0:T(8,128)(2,1)S(1)} %get-tuple-element.24.own_pos), channel_id=1, source_target_pairs={{0,112},{16,0},{32,16},{48,32},{64,48},{80,64},{96,80},{112,96},{1... | collective-permute-start | bytes 36872 | tf_op jit(solution)/shard_map/ppermute | solution.py:479
  15.2 7.1 %collective-permute-start.2 = (bf16[3,16,128]{2,1,0:T(8,128)(2,1)S(1)}, bf16[3,16,128]{2,1,0:T(8,128)(2,1)S(1)}, u32[]{:S(2)}, u32[]{:S(2)}) collective-permute-start(bf16[3,16,128]{2,1,0:T(8,128)(2,1)S(1)} %get-tuple-element.24.own_pos), channel_id=1, source_target_pairs={{0,16},{16,32},{32,48},{48,64},{64,80},{80,96},{96,112},{112,0},{1... | collective-permute-start | bytes 36872 | tf_op jit(solution)/shard_map/ppermute | solution.py:478
  38.1 23.2 %all-to-all-start.1 = ((bf16[16,256,128]{2,1,0:T(8,128)(2,1)}), bf16[16,256,128]{2,1,0:T(8,128)(2,1)S(1)}, u32[]{:S(2)}, u32[]{:S(2)}) async-start(bf16[16,256,128]{2,1,0:T(8,128)(2,1)} %bitcast.37), calls=%async_computation.1 | async-start | bytes 2097152 | tf_op jit(solution)/shard_map/all_to_all | solution.py:516
  76.1 19.4 %all-to-all-start.2 = ((bf16[16,256,128]{2,1,0:T(8,128)(2,1)}), bf16[16,256,128]{2,1,0:T(8,128)(2,1)S(1)}, u32[]{:S(2)}, u32[]{:S(2)}) async-start(bf16[16,256,128]{2,1,0:T(8,128)(2,1)} %bitcast.7), calls=%async_computation.2 | async-start | bytes 2097152 | tf_op jit(solution)/shard_map/all_to_all | solution.py:557
